TPU v7x, 32 devices: a whole 2x2x4 slice. The times are simulated.
32 devices in a mesh: groups: 1, ctx: 16 (over z, y, x), exp: 2 (over core).
Axes of the slice: x: 2, y: 2, z: 4, core: 2. Of those that a mesh axis runs over, the one named last changes fastest.
Arguments:
- queries: bfloat16 [2048, 2048], P(('groups', 'ctx'), 'exp'), may hold values from -40 to 40
- key_rows: bfloat16 [2048, 256], P(('groups', 'ctx'), 'exp'), may hold values from -15 to 15
- value_rows: bfloat16 [2048, 256], P(('groups', 'ctx'), 'exp'), may hold values from -6 to 6
- hidden_in: bfloat16 [2048, 1024], P(('groups', 'ctx')), may hold values from -40 to 40
- out_proj: bfloat16 [2048, 1024], P('exp'), may hold values from -0.125 to 0.125
- norm_gain: float32 [1024], replicated, may hold values from 0.1 to 1.9
- expert_ids: int32 [2048, 8], P(('groups', 'ctx')), may hold values from 0 to 15, all different within a row; in each aligned block of 128 rows (0 to 127, 128 to 255, ...) at most 96 rows name the same one
- gate_scores: float32 [2048, 8], P(('groups', 'ctx')), may hold values from 0.05 to 1
- w_gate: bfloat16 [16, 1024, 384], P('ctx'), may hold values from -0.1875 to 0.1875
- w_up: bfloat16 [16, 1024, 384], P('ctx'), may hold values from -0.1875 to 0.1875
- w_down: bfloat16 [16, 384, 1024], P('ctx'), may hold values from -0.3125 to 0.3125
Outputs:
- layer_out: bfloat16 [2048, 1024], P(('groups', 'ctx'), 'exp')
Inputs may be any that keep to these rules, and one draw needn't show every extreme that they name: `expert_ids`: each row names 8 different experts. No expert is named by more than 96 rows of one aligned block of 128 rows, a bound that some block reaches.
All inputs are finite; a program needn't handle non-finite values.
Results may differ from a plain program's by a relative error of at most 0.0035.
Values may be sent and summed in bfloat16 or wider, within the bound.
No kernel may reach another device: no remote copies, remote signals or barrier semaphores. Data moves between devices by JAX's collectives and lax.ppermute only.
A program may use at most 64 MiB of HBM per device.

v0:
```python
import math
import jax
import jax.numpy as jnp
from jax import lax
from jax.sharding import PartitionSpec as P


def attend(queries, key_rows, value_rows, first):
    token_count = queries.shape[0]
    kv_heads = key_rows.shape[1] // 128
    q_heads = queries.shape[1] // 128
    group = q_heads // kv_heads
    grouped = queries.reshape(token_count, kv_heads, group, 128)
    query_pos = first + jnp.arange(token_count, dtype=jnp.int32)
    last_pos = first + token_count - 1
    scale = 128 ** (-0.5)
    shape_rows = (kv_heads, group, token_count)
    start_state = (
        jnp.full(shape_rows, -1e30, jnp.float32),
        jnp.zeros(shape_rows, jnp.float32),
        jnp.zeros(shape_rows + (128,), jnp.float32),
    )
    key_piece = lax.all_gather(key_rows, "ctx", axis=0, tiled=True)
    value_piece = lax.all_gather(value_rows, "ctx", axis=0, tiled=True)
    count = key_piece.shape[0]
    width = math.gcd(count, 512)

    def step(block_index, state):
        offset = block_index * width

        def compute(inner):
            running_max, running_sum, accum = inner
            key_block = lax.dynamic_slice_in_dim(key_piece, block_index * width, width, 0).reshape(
                width, kv_heads, 128
            )
            value_block = lax.dynamic_slice_in_dim(
                value_piece, block_index * width, width, 0
            ).reshape(width, kv_heads, 128)
            scores = (
                jnp.einsum("tkgd,skd->kgts", grouped, key_block, preferred_element_type=jnp.float32)
                * scale
            )
            key_pos = offset + jnp.arange(width, dtype=jnp.int32)
            allowed = key_pos[None, :] <= query_pos[:, None]
            scores = jnp.where(allowed, scores, -jnp.inf)
            new_max = jnp.maximum(running_max, jnp.max(scores, axis=-1))
            factor = jnp.exp(running_max - new_max)
            weights = jnp.exp(scores - new_max[..., None])
            new_sum = running_sum * factor + jnp.sum(weights, axis=-1)
            product = jnp.einsum(
                "kgts,skd->kgtd",
                weights.astype(jnp.bfloat16),
                value_block,
                preferred_element_type=jnp.float32,
            )
            return (new_max, new_sum, accum * factor[..., None] + product)

        return lax.cond(offset <= last_pos, compute, lambda inner: inner, state)

    _, total, accum = lax.fori_loop(0, count // width, step, start_state)
    output = accum / total[..., None]
    return (
        jnp.transpose(output, (2, 0, 1, 3)).reshape(token_count, q_heads * 128).astype(jnp.bfloat16)
    )


def place_rows(expert_ids, sent_rows, capacity, expert_count):
    top_count = expert_ids.shape[1]
    flat_ids = expert_ids.reshape(-1)
    onehot = (flat_ids[:, None] == jnp.arange(expert_count, dtype=jnp.int32)[None, :]).astype(
        jnp.int32
    )
    earlier = jnp.cumsum(onehot, axis=0) - onehot
    slot_index = jnp.sum(earlier * onehot, axis=1)
    destination = flat_ids * capacity + slot_index
    copies = jnp.repeat(sent_rows, top_count, axis=0)
    buffer = (
        jnp.zeros((expert_count * capacity, sent_rows.shape[1]), sent_rows.dtype)
        .at[destination]
        .set(copies)
    )
    return (buffer.reshape(expert_count, 2, capacity // 2, sent_rows.shape[1]), destination)


def per_device(
    queries,
    key_rows,
    value_rows,
    hidden_in,
    out_proj,
    norm_gain,
    expert_ids,
    gate_scores,
    w_gate,
    w_up,
    w_down,
):
    token_count = queries.shape[0]
    model_width = hidden_in.shape[1]
    half_width = model_width // 2
    ctx_size = lax.axis_size("ctx")
    local_experts = w_gate.shape[0]
    expert_count = local_experts * ctx_size
    top_count = expert_ids.shape[1]
    capacity = 2 * (
        min(token_count, max(2, 3 * token_count * top_count // (2 * expert_count))) // 2
    )
    half_cap = capacity // 2
    first = lax.axis_index("ctx") * token_count
    core = lax.axis_index("exp")
    side_start = core * half_width
    attended = attend(queries, key_rows, value_rows, first)
    head_part = jnp.dot(attended, out_proj, preferred_element_type=jnp.float32)
    attn_full = lax.psum(head_part.astype(jnp.bfloat16), "exp").astype(jnp.float32)
    resid = hidden_in.astype(jnp.float32) + attn_full
    inverse = lax.rsqrt(jnp.mean(resid * resid, axis=1, keepdims=True) + 1e-06)
    sent_rows = (resid * inverse * norm_gain[None, :]).astype(jnp.bfloat16)
    resid_half = lax.dynamic_slice_in_dim(resid, side_start, half_width, 1)
    buffer, destination = place_rows(expert_ids, sent_rows, capacity, expert_count)
    own_slots = lax.dynamic_slice_in_dim(buffer, core, 1, 1)
    grouped = lax.all_to_all(own_slots, "ctx", split_axis=0, concat_axis=0, tiled=True)
    gate = jnp.einsum("sxmd,xdf->sxmf", grouped, w_gate, preferred_element_type=jnp.float32)
    upper = jnp.einsum("sxmd,xdf->sxmf", grouped, w_up, preferred_element_type=jnp.float32)
    hidden = (jax.nn.silu(gate) * upper).astype(jnp.bfloat16)
    partial_value = jnp.einsum(
        "sxmf,xfd->sxmd", hidden, w_down, preferred_element_type=jnp.float32
    ).astype(jnp.bfloat16)
    returned = lax.all_to_all(partial_value, "ctx", split_axis=0, concat_axis=0, tiled=True)
    flat_back = returned.reshape(expert_count * half_cap, model_width)
    slot_of = destination % capacity
    expert_of = destination // capacity
    owned = slot_of // half_cap == core
    local_index = jnp.where(owned, expert_of * half_cap + slot_of - core * half_cap, 0)
    picked = flat_back[local_index].astype(jnp.float32)
    mixing = (gate_scores / jnp.sum(gate_scores, axis=1, keepdims=True)).reshape(-1)
    mixing = jnp.where(owned, mixing, 0.0)
    weighted = (picked * mixing[:, None]).reshape(token_count, top_count, model_width)
    mixed_part = jnp.sum(weighted, axis=1)
    moe_half = lax.psum_scatter(
        mixed_part.astype(jnp.bfloat16), "exp", scatter_dimension=1, tiled=True
    ).astype(jnp.float32)
    return (resid_half + moe_half).astype(jnp.bfloat16)


def solution(mesh):
    placed = (
        P(("groups", "ctx"), "exp"),
        P(("groups", "ctx"), "exp"),
        P(("groups", "ctx"), "exp"),
        P(("groups", "ctx"), None),
        P("exp", None),
        P(),
        P(("groups", "ctx"), None),
        P(("groups", "ctx"), None),
        P("ctx", None, None),
        P("ctx", None, None),
        P("ctx", None, None),
    )
    return jax.shard_map(
        per_device,
        mesh=mesh,
        in_specs=placed,
        out_specs=P(("groups", "ctx"), "exp"),
        check_vma=False,
    )
```

profile of v0, /device:TPU:0, one launch (start us, length us, event | category | flops | bytes accessed | tf_op | source)
XLA Modules:
  0.0 254.2 jit_solution(11516045207703964452)
XLA Ops:
  6.5 0.0 copy-start
  6.5 0.0 all-reduce.2.cloned.1.call-start
  6.5 45.7 %all_gather.6 = bf16[2048,128]{1,0:T(8,128)(2,1)S(1)} all-gather(bf16[128,128]{1,0:T(8,128)(2,1)} %param.16), channel_id=1, replica_groups=mesh['groups'=1,'ctx'=16,'exp'=2] {'ctx'}, dimensions={0}, use_global_device_ids=true | all-gather | bytes 557056 | tf_op jit(solution)/shard_map/all_gather | solution.py:23
  52.2 40.9 %all_gather.7 = bf16[2048,128]{1,0:T(8,128)(2,1)} all-gather(bf16[128,128]{1,0:T(8,128)(2,1)} %param.17), channel_id=1, replica_groups=mesh['groups'=1,'ctx'=16,'exp'=2] {'ctx'}, dimensions={0}, use_global_device_ids=true | all-gather | bytes 557056 | tf_op jit(solution)/shard_map/all_gather | solution.py:24
  93.1 1.1 copy.47
  94.2 0.2 copy.48
  94.5 2.8 %while.18 = (s32[]{:T(128)}, f32[1,8,128]{2,1,0:T(8,128)S(1)}, f32[1,8,128]{2,1,0:T(8,128)S(1)}, f32[1,8,128,128]{3,2,1,0:T(8,128)S(1)}, s32[]{:T(128)}, /*index...) while((s32[]{:T(128)}, f32[1,8,128]{2,1,0:T(8,128)S(1)}, ...), condition=%wide.region_5.6_spmd.clone, body=%wide.region_0.5_spmd.clone.sunk | while | flops 272436864 | bytes 8067405 | solution.py:60
  94.5 2.6 %conditional.3 = ((f32[1,8,128]{2,1,0:T(8,128)S(1)}, f32[1,8,128]{2,1,0:T(8,128)S(1)}, f32[1,8,128,128]{3,2,1,0:T(8,128)S(1)})) conditional(s32[]{:T(128)} %convert_element_type.120, (f32[1,8,128]{2,1,0:T(8,128)S(1)}, f32[1,8,128]{2,1,0:T(8,128)S(1)}, f32[1,8,128,128]{3,2,1,0:T(8,128)S(1)}) %tuple.49, (s32[]{:T(128)}, s32[]{:T(128)}, s32[]{:T(128)}, ...), branch_computations={%region_1.0_spmd, %region_2.4_spmd} | conditional | flops 272436864 | bytes 8066654 | solution.py:58
  94.6 0.1 broadcast_compare_fusion
  94.7 0.4 fusion.55
  95.2 1.6 fusion.4
  96.8 0.3 fusion.3
  97.3 0.2 copy.49
  97.5 0.0 copy-start.3
  97.5 0.1 divide_convert_fusion
  97.6 0.0 copy-start.2
  97.6 0.0 copy-done
  97.6 0.0 copy-start.5
  97.6 1.2 convolution_convert_fusion.1
  98.8 0.0 all-reduce.2.cloned.1.call-update
  98.8 0.0 copy-done.3
  98.8 0.1 copy.51
  98.9 0.1 eq.51
  99.0 0.1 eq.47
  99.1 4.5 %reduce-window.6 = s32[16,8,128]{2,1,0:T(8,128)S(1)} reduce-window(s32[16,8,128]{2,1,0:T(8,128)S(1)} %fusion.51, s32[]{:T(128)} %constant.82.clone.1), window={size=1x1x128 pad=0_0x0_0x127_0}, to_apply=%region_7.8 | reduce-window | flops 2080768 | bytes 131076 | tf_op jit(solution)/shard_map/reduce-window
  103.7 0.1 slice.10
  103.7 0.1 copy.53
  103.9 0.1 copy.54
  104.0 0.1 broadcast_add_fusion.1
  104.1 0.1 copy.50
  104.2 0.1 mul.120
  104.3 0.1 compare_select_fusion
  104.4 18.4 %all-reduce.2.cloned.1.call-done = bf16[128,1024]{1,0:T(8,128)(2,1)} async-done(((bf16[128,1024]{1,0:T(8,128)(2,1)}), bf16[128,1024]{1,0:T(8,128)(2,1)}) %all-reduce.2.cloned.1.call-update) | async-done | bytes 262160 | tf_op jit(solution)/shard_map/psum | solution.py:114
  122.8 0.0 copy-done.2
  122.8 1.1 convert_add_fusion
  123.9 0.0 copy-done.5
  123.9 1.1 multiply_convert_fusion
  125.0 7.4 %scatter_custom_fusion = bf16[1536,1024]{1,0:T(8,128)(2,1)} fusion(s32[1024]{0:T(1024)S(1)} %bitcast.140, bf16[]{:T(256)} %constant.91.clone.1, bf16[128,1024]{1,0:T(8,128)(2,1)S(1)} %multiply_convert_fusion), kind=kCustom, calls=%fused_computation.27 | custom fusion | bytes 3407874 | tf_op jit(solution)/shard_map/scatter | solution.py:80
  132.4 1.6 constant_dynamic-slice_fusion
  133.9 0.0 copy-start.6
  133.9 44.7 %all_to_all.10 = bf16[16,1,48,1024]{3,2,1,0:T(8,128)(2,1)S(1)} all-to-all(bf16[16,1,48,1024]{3,2,1,0:T(8,128)(2,1)S(1)} %constant_dynamic-slice_fusion), channel_id=1, replica_groups=mesh['groups'=1,'ctx'=16,'exp'=2] {'ctx'}, dimensions={0} | all-to-all | bytes 3145728 | tf_op jit(solution)/shard_map/all_to_all | solution.py:121
  178.7 0.0 copy-start.1
  178.7 1.1 copy-done.1
  179.8 0.0 copy-done.6
  179.8 2.0 fusion.25
  181.8 5.2 %fusion.24 = bf16[16,1,48,1024]{3,2,1,0:T(8,128)(2,1)} fusion(bf16[16,1,48,1024]{3,2,1,0:T(8,128)(2,1)} %copy-done.1, f32[16,1,48,384]{3,2,0,1:T(8,128)} %fusion.25, bf16[1,384,1024]{2,1,0:T(8,128)(2,1)} %param.25, bf16[1,1024,384]{2,1,0:T(8,128)(2,1)} %param.24), kind=kOutput, calls=%fused_computation.35 | convolution fusion | flops 1210515456 | bytes 5898240 | tf_op jit(solution)/shard_map/sxmf,xfd->sxmd/dot_general | solution.py:125
  187.0 0.0 copy-start.4
  187.0 4.5 %all-to-all-start.1 = ((bf16[16,1,48,1024]{3,2,1,0:T(8,128)(2,1)}), bf16[16,1,48,1024]{3,2,1,0:T(8,128)(2,1)}, u32[]{:S(2)}, u32[]{:S(2)}) async-start(bf16[16,1,48,1024]{3,2,1,0:T(8,128)(2,1)} %fusion.24), calls=%async_computation.1 | async-start | bytes 3145728 | tf_op jit(solution)/shard_map/all_to_all | solution.py:128
  191.5 0.2 reduce-scatter.2.cloned.1.call-start
  191.8 0.1 reduce_sum.54
  191.9 0.0 copy-done.4
  192.0 0.1 copy.57
  192.1 32.7 %all-to-all-done.1 = bf16[16,1,48,1024]{3,2,1,0:T(8,128)(2,1)} async-done(((bf16[16,1,48,1024]{3,2,1,0:T(8,128)(2,1)}), bf16[16,1,48,1024]{3,2,1,0:T(8,128)(2,1)}, u32[]{:S(2)}, u32[]{:S(2)}) %all-to-all-start.1) | async-done | bytes 1572896 | tf_op jit(solution)/shard_map/all_to_all | solution.py:128
  224.8 7.6 %gather_fusion = bf16[1024,1024]{1,0:T(8,128)(2,1)} fusion(bf16[768,1024]{1,0:T(8,128)(2,1)} %bitcast.41, s32[1024]{0:T(1024)S(1)} %broadcast_clamp_fusion), kind=kCustom, calls=%fused_computation | custom fusion | bytes 4198400 | tf_op jit(solution)/shard_map/gather | solution.py:134
  232.4 3.7 %fusion.16 = bf16[128,1024]{1,0:T(8,128)(2,1)} fusion(bf16[1024,1024]{1,0:T(8,128)(2,1)} %gather_fusion, f32[128,8]{1,0:T(8,128)S(1)} %copy.57), kind=kLoop, calls=%fused_computation.26 | loop fusion | flops 3014656 | bytes 2363392 | tf_op jit(solution)/shard_map/reduce_sum | solution.py:138
  236.1 0.0 reduce-scatter.2.cloned.1.call-update
  236.1 9.7 %reduce-scatter.2.cloned.1.call-done = bf16[128,512]{1,0:T(8,128)(2,1)} async-done(((bf16[128,1024]{1,0:T(8,128)(2,1)}), bf16[128,512]{1,0:T(8,128)(2,1)}) %reduce-scatter.2.cloned.1.call-update) | async-done | bytes 131088 | tf_op jit(solution)/shard_map/reduce_scatter | solution.py:139
  245.8 1.6 add_convert_fusion
  (25 shorter events, 0.3 us)
Async XLA Ops:
  6.5 91.1 %copy-start = (bf16[1024,1024]{1,0:T(8,128)(2,1)S(1)}, bf16[1024,1024]{1,0:T(8,128)(2,1)}, u32[]{:S(2)}) copy-start(bf16[1024,1024]{1,0:T(8,128)(2,1)} %param.19) | copy-start | bytes 6291460
  6.5 116.2 %all-reduce.2.cloned.1.call-start = ((), (), s32[]{:S(2)}) async-start(), calls=%async_computation.3 | async-start | bytes 524288 | tf_op jit(solution)/shard_map/psum | solution.py:114
  97.5 1.3 copy-start.3
  97.6 25.2 %copy-start.2 = (bf16[128,1024]{1,0:T(8,128)(2,1)S(1)}, bf16[128,1024]{1,0:T(8,128)(2,1)}, u32[]{:S(2)}) copy-start(bf16[128,1024]{1,0:T(8,128)(2,1)} %param.18) | copy-start | bytes 786436
  97.6 26.3 %copy-start.5 = (f32[1024]{0:T(1024)S(1)}, f32[1024]{0:T(1024)}, u32[]{:S(2)}) copy-start(f32[1024]{0:T(1024)} %param.20) | copy-start | bytes 12292
  133.9 45.9 %copy-start.6 = (bf16[1,1024,384]{2,1,0:T(8,128)(2,1)S(1)}, bf16[1,1024,384]{2,1,0:T(8,128)(2,1)}, u32[]{:S(2)}) copy-start(bf16[1,1024,384]{2,1,0:T(8,128)(2,1)} %param.23) | copy-start | bytes 2359300
  178.7 1.1 copy-start.1
  187.0 4.9 %copy-start.4 = (f32[128,8]{0,1:T(8,128)S(1)}, f32[128,8]{0,1:T(8,128)}, u32[]{:S(2)}) copy-start(f32[128,8]{0,1:T(8,128)} %param.22) | copy-start | bytes 12292
  187.0 37.8 %all-to-all-start.1 = ((bf16[16,1,48,1024]{3,2,1,0:T(8,128)(2,1)}), bf16[16,1,48,1024]{3,2,1,0:T(8,128)(2,1)}, u32[]{:S(2)}, u32[]{:S(2)}) async-start(bf16[16,1,48,1024]{3,2,1,0:T(8,128)(2,1)} %fusion.24), calls=%async_computation.1 | async-start | bytes 3145728 | tf_op jit(solution)/shard_map/all_to_all | solution.py:128
  191.5 54.3 %reduce-scatter.2.cloned.1.call-start = ((), (), s32[]{:S(2)}) async-start(), calls=%async_computation.4 | async-start | bytes 393216 | tf_op jit(solution)/shard_map/reduce_scatter | solution.py:139
Sparse Core Ops, SparseCore 0:
  98.9 23.7 all-reduce.1
  236.3 9.4 reduce-scatter.1
where the time goes:
time: 255 us; the launch traced here: 254 us
  blocking collectives  131 us (51%)
  waiting for transfers between devices  60.8 us (24%)
  local copies, waits for them, and re-layouts  20.3 us (8%)
  between operations  13.6 us (5%)
  other arithmetic  12.8 us (5%)
  matrix products  10.4 us (4%)
  starting transfers between devices  4.76 us (2%)
    all_gather x1, blocking collectives, attend(): key_piece = lax.all_gather(key_rows, 'ctx', axis=0, tiled=True)  45.7 us
    all_to_all x1, blocking collectives, per_device(): lax.all_to_all(own_slots, 'ctx', split_axis=0, concat_axis=0, tiled=True)  44.7 us
    all_gather x1, blocking collectives, attend(): value_piece = lax.all_gather(value_rows, 'ctx', axis=0, tiled=True)  40.9 us
    all_to_all x1, waiting for transfers between devices, per_device(): lax.all_to_all(partial_value, 'ctx', split_axis=0, concat_axis=0, tiled=T...  32.7 us
    psum x1, waiting for transfers between devices, per_device(): lax.psum(head_part.astype(jnp.bfloat16), 'exp').astype(jnp.float32)  18.4 us
    reduce_scatter x1, waiting for transfers between devices, per_device(): lax.psum_scatter(mixed_part.astype(jnp.bfloat16), 'exp', scatter_dimensio...  9.66 us
    gather x1, local copies, waits for them, and re-layouts, per_device(): picked = flat_back[local_index].astype(jnp.float32)  7.65 us
    scatter x1, local copies, waits for them, and re-layouts, place_rows(): buffer = jnp.zeros((expert_count * capacity, sent_rows.shape[1]), sent_ro...  7.39 us
  transfers between devices with their start and end apart: 3, of which 3 were waited for; matrix products, arithmetic and copies ran while one was open for 2% of the time, Pallas kernels for 0%

commit v1 on v0

--- a/solution.py
+++ b/solution.py
@@ -3,6 +3,12 @@
 import jax.numpy as jnp
 from jax import lax
 from jax.sharding import PartitionSpec as P
+
+
+def summed_here(x, axis):
+    shards = lax.all_gather(x, axis, axis=0, tiled=False)
+    total = shards.sum(axis=0)
+    return total
 
 
 def attend(queries, key_rows, value_rows, first):
@@ -111,7 +117,7 @@
     side_start = core * half_width
     attended = attend(queries, key_rows, value_rows, first)
     head_part = jnp.dot(attended, out_proj, preferred_element_type=jnp.float32)
-    attn_full = lax.psum(head_part.astype(jnp.bfloat16), "exp").astype(jnp.float32)
+    attn_full = summed_here(head_part.astype(jnp.bfloat16), "exp").astype(jnp.float32)
     resid = hidden_in.astype(jnp.float32) + attn_full
     inverse = lax.rsqrt(jnp.mean(resid * resid, axis=1, keepdims=True) + 1e-06)
     sent_rows = (resid * inverse * norm_gain[None, :]).astype(jnp.bfloat16)

time: 255 us -> 242 us (0.949)
  waiting for transfers between devices: 60.8 us -> 42.4 us
  blocking collectives: 131 us -> 138 us
    psum x1 -> x0, waiting for transfers between devices: 18.4 us -> none  [per_device(): lax.psum(head_part.astype(jnp.bfloat16), 'exp').astype(jnp.float32)]
    all_to_all x1, blocking collectives: 44.7 us -> 49 us  [per_device(): lax.all_to_all(own_slots, 'ctx', split_axis=0, concat_axis=0, tiled=True)]
  transfers between devices with their start and end apart: 3 -> 2, of which waited for: 3 -> 2; matrix products, arithmetic and copies ran while one was open for 2% -> 0% of each run, Pallas kernels for 0% -> 0%
where the time goes in v1:
time: 242 us; the launch traced here: 241 us
  blocking collectives  138 us (57%)
  waiting for transfers between devices  42.4 us (18%)
  local copies, waits for them, and re-layouts  21.2 us (9%)
  between operations  13.6 us (6%)
  other arithmetic  11.7 us (5%)
  matrix products  9.73 us (4%)
  starting transfers between devices  4.76 us (2%)
    all_to_all x1, blocking collectives, per_device(): lax.all_to_all(own_slots, 'ctx', split_axis=0, concat_axis=0, tiled=True)  49 us
    all_gather x1, blocking collectives, attend(): key_piece = lax.all_gather(key_rows, 'ctx', axis=0, tiled=True)  45.6 us
    all_gather x1, blocking collectives, attend(): value_piece = lax.all_gather(value_rows, 'ctx', axis=0, tiled=True)  40.9 us
    all_to_all x1, waiting for transfers between devices, per_device(): lax.all_to_all(partial_value, 'ctx', split_axis=0, concat_axis=0, tiled=T...  32.7 us
    reduce_scatter x1, waiting for transfers between devices, per_device(): lax.psum_scatter(mixed_part.astype(jnp.bfloat16), 'exp', scatter_dimensio...  9.66 us
    gather x1, local copies, waits for them, and re-layouts, per_device(): picked = flat_back[local_index].astype(jnp.float32)  7.65 us
    scatter x1, local copies, waits for them, and re-layouts, place_rows(): buffer = jnp.zeros((expert_count * capacity, sent_rows.shape[1]), sent_ro...  7.39 us
    dot_general x1, matrix products, per_device(): jnp.einsum('sxmf,xfd->sxmd', hidden, w_down, preferred_element_type=jnp.f...  5.18 us
  transfers between devices with their start and end apart: 2, of which 2 were waited for; matrix products, arithmetic and copies ran while one was open for 0% of the time, Pallas kernels for 0%

profile of v1, /device:TPU:0, one launch (start us, length us, event | category | flops | bytes accessed | tf_op | source)
XLA Modules:
  0.0 241.1 jit_solution(6577635150976122261)
XLA Ops:
  6.5 0.0 copy-start
  6.5 0.9 copy.51
  7.5 0.1 eq.51
  7.6 0.1 eq.47
  7.7 0.7 broadcast_multiply_fusion
  8.3 45.6 %all_gather.12 = bf16[2048,128]{1,0:T(8,128)(2,1)S(1)} all-gather(bf16[128,128]{1,0:T(8,128)(2,1)} %param.16), channel_id=1, replica_groups=mesh['groups'=1,'ctx'=16,'exp'=2] {'ctx'}, dimensions={0}, use_global_device_ids=true | all-gather | bytes 557056 | tf_op jit(solution)/shard_map/all_gather | solution.py:29
  53.9 40.9 %all_gather.13 = bf16[2048,128]{1,0:T(8,128)(2,1)} all-gather(bf16[128,128]{1,0:T(8,128)(2,1)} %param.17), channel_id=1, replica_groups=mesh['groups'=1,'ctx'=16,'exp'=2] {'ctx'}, dimensions={0}, use_global_device_ids=true | all-gather | bytes 557056 | tf_op jit(solution)/shard_map/all_gather | solution.py:30
  94.8 1.1 copy.47
  95.9 0.2 copy.48
  96.2 2.8 %while.18 = (s32[]{:T(128)}, f32[1,8,128]{2,1,0:T(8,128)S(1)}, f32[1,8,128]{2,1,0:T(8,128)S(1)}, f32[1,8,128,128]{3,2,1,0:T(8,128)S(1)}, s32[]{:T(128)}, /*index...) while((s32[]{:T(128)}, f32[1,8,128]{2,1,0:T(8,128)S(1)}, ...), condition=%wide.region_5.6_spmd.clone, body=%wide.region_0.5_spmd.clone.sunk | while | flops 272436864 | bytes 8067405 | solution.py:66
  96.2 2.6 %conditional.3 = ((f32[1,8,128]{2,1,0:T(8,128)S(1)}, f32[1,8,128]{2,1,0:T(8,128)S(1)}, f32[1,8,128,128]{3,2,1,0:T(8,128)S(1)})) conditional(s32[]{:T(128)} %convert_element_type.122, (f32[1,8,128]{2,1,0:T(8,128)S(1)}, f32[1,8,128]{2,1,0:T(8,128)S(1)}, f32[1,8,128,128]{3,2,1,0:T(8,128)S(1)}) %tuple.49, (s32[]{:T(128)}, s32[]{:T(128)}, s32[]{:T(128)}, ...), branch_computations={%region_1.0_spmd, %region_2.4_spmd} | conditional | flops 272436864 | bytes 8066654 | solution.py:64
  96.2 0.1 broadcast_compare_fusion
  96.4 0.4 fusion.55
  96.8 1.6 fusion.4
  98.5 0.3 fusion.3
  99.0 0.2 copy.49
  99.2 0.1 divide_convert_fusion
  99.2 0.0 copy-done
  99.2 0.0 copy-start.2
  99.3 0.5 convolution_convert_fusion.1
  99.7 0.0 copy-start.5
  99.8 2.2 all-gather
  101.9 0.1 reduce_sum.63
  102.0 0.0 copy-done.2
  102.0 0.2 convert_add_fusion
  102.2 4.5 %reduce-window.6 = s32[16,8,128]{2,1,0:T(8,128)S(1)} reduce-window(s32[16,8,128]{2,1,0:T(8,128)S(1)} %fusion.51, s32[]{:T(128)} %constant.83.clone.1), window={size=1x1x128 pad=0_0x0_0x127_0}, to_apply=%region_7.8 | reduce-window | flops 2080768 | bytes 131076 | tf_op jit(solution)/shard_map/reduce-window
  106.8 0.1 slice.10
  106.8 0.1 copy.53
  107.0 0.1 copy.54
  107.1 0.1 broadcast_add_fusion.1
  107.2 0.1 copy.50
  107.3 0.1 mul.120
  107.4 0.0 copy-done.5
  107.4 0.1 multiply_convert_fusion
  107.5 0.1 compare_select_fusion
  107.6 7.4 %scatter_custom_fusion = bf16[1536,1024]{1,0:T(8,128)(2,1)} fusion(s32[1024]{0:T(1024)S(1)} %bitcast.142, bf16[]{:T(256)} %constant.90.clone.1, bf16[128,1024]{1,0:T(8,128)(2,1)S(1)} %multiply_convert_fusion), kind=kCustom, calls=%fused_computation.27 | custom fusion | bytes 3407874 | tf_op jit(solution)/shard_map/scatter | solution.py:86
  115.0 1.6 constant_dynamic-slice_fusion
  116.6 0.0 copy-start.6
  116.6 49.0 %all_to_all.10 = bf16[16,1,48,1024]{3,2,1,0:T(8,128)(2,1)S(1)} all-to-all(bf16[16,1,48,1024]{3,2,1,0:T(8,128)(2,1)S(1)} %constant_dynamic-slice_fusion), channel_id=1, replica_groups=mesh['groups'=1,'ctx'=16,'exp'=2] {'ctx'}, dimensions={0} | all-to-all | bytes 3145728 | tf_op jit(solution)/shard_map/all_to_all | solution.py:127
  165.6 0.0 copy-start.1
  165.6 1.1 copy-done.1
  166.7 0.0 copy-done.6
  166.7 2.0 fusion.25
  168.7 5.2 %fusion.24 = bf16[16,1,48,1024]{3,2,1,0:T(8,128)(2,1)} fusion(bf16[16,1,48,1024]{3,2,1,0:T(8,128)(2,1)} %copy-done.1, f32[16,1,48,384]{3,2,0,1:T(8,128)} %fusion.25, bf16[1,384,1024]{2,1,0:T(8,128)(2,1)} %param.25, bf16[1,1024,384]{2,1,0:T(8,128)(2,1)} %param.24), kind=kOutput, calls=%fused_computation.35 | convolution fusion | flops 1210515456 | bytes 5898240 | tf_op jit(solution)/shard_map/sxmf,xfd->sxmd/dot_general | solution.py:131
  173.9 0.0 copy-start.4
  173.9 0.0 copy-start.3
  173.9 4.5 %all-to-all-start.1 = ((bf16[16,1,48,1024]{3,2,1,0:T(8,128)(2,1)}), bf16[16,1,48,1024]{3,2,1,0:T(8,128)(2,1)}, u32[]{:S(2)}, u32[]{:S(2)}) async-start(bf16[16,1,48,1024]{3,2,1,0:T(8,128)(2,1)} %fusion.24), calls=%async_computation.1 | async-start | bytes 3145728 | tf_op jit(solution)/shard_map/all_to_all | solution.py:134
  178.4 0.2 reduce-scatter.2.cloned.1.call-start
  178.7 0.1 reduce_sum.67
  178.8 0.0 copy-done.4
  178.8 0.0 copy-done.3
  178.9 0.1 copy.57
  179.0 32.7 %all-to-all-done.1 = bf16[16,1,48,1024]{3,2,1,0:T(8,128)(2,1)} async-done(((bf16[16,1,48,1024]{3,2,1,0:T(8,128)(2,1)}), bf16[16,1,48,1024]{3,2,1,0:T(8,128)(2,1)}, u32[]{:S(2)}, u32[]{:S(2)}) %all-to-all-start.1) | async-done | bytes 1572896 | tf_op jit(solution)/shard_map/all_to_all | solution.py:134
  211.7 7.6 %gather_fusion = bf16[1024,1024]{1,0:T(8,128)(2,1)} fusion(bf16[768,1024]{1,0:T(8,128)(2,1)} %bitcast.42, s32[1024]{0:T(1024)S(1)} %broadcast_clamp_fusion), kind=kCustom, calls=%fused_computation | custom fusion | bytes 4198400 | tf_op jit(solution)/shard_map/gather | solution.py:140
  219.4 3.7 %fusion.16 = bf16[128,1024]{1,0:T(8,128)(2,1)} fusion(bf16[1024,1024]{1,0:T(8,128)(2,1)} %gather_fusion, f32[128,8]{1,0:T(8,128)S(1)} %copy.57), kind=kLoop, calls=%fused_computation.26 | loop fusion | flops 3014656 | bytes 2363392 | tf_op jit(solution)/shard_map/reduce_sum | solution.py:144
  223.0 0.0 reduce-scatter.2.cloned.1.call-update
  223.1 9.7 %reduce-scatter.2.cloned.1.call-done = bf16[128,512]{1,0:T(8,128)(2,1)} async-done(((bf16[128,1024]{1,0:T(8,128)(2,1)}), bf16[128,512]{1,0:T(8,128)(2,1)}) %reduce-scatter.2.cloned.1.call-update) | async-done | bytes 131088 | tf_op jit(solution)/shard_map/reduce_scatter | solution.py:145
  232.7 1.6 add_convert_fusion
  (24 shorter events, 0.3 us)
Async XLA Ops:
  6.5 92.7 %copy-start = (bf16[1024,1024]{1,0:T(8,128)(2,1)S(1)}, bf16[1024,1024]{1,0:T(8,128)(2,1)}, u32[]{:S(2)}) copy-start(bf16[1024,1024]{1,0:T(8,128)(2,1)} %param.19) | copy-start | bytes 6291460
  99.2 2.8 %copy-start.2 = (bf16[128,1024]{1,0:T(8,128)(2,1)S(1)}, bf16[128,1024]{1,0:T(8,128)(2,1)}, u32[]{:S(2)}) copy-start(bf16[128,1024]{1,0:T(8,128)(2,1)} %param.18) | copy-start | bytes 786436
  99.7 7.6 %copy-start.5 = (f32[1024]{0:T(1024)S(1)}, f32[1024]{0:T(1024)}, u32[]{:S(2)}) copy-start(f32[1024]{0:T(1024)} %param.20) | copy-start | bytes 12292
  116.6 50.1 %copy-start.6 = (bf16[1,1024,384]{2,1,0:T(8,128)(2,1)S(1)}, bf16[1,1024,384]{2,1,0:T(8,128)(2,1)}, u32[]{:S(2)}) copy-start(bf16[1,1024,384]{2,1,0:T(8,128)(2,1)} %param.23) | copy-start | bytes 2359300
  165.6 1.1 copy-start.1
  173.9 4.9 %copy-start.4 = (f32[128,8]{0,1:T(8,128)S(1)}, f32[128,8]{0,1:T(8,128)}, u32[]{:S(2)}) copy-start(f32[128,8]{0,1:T(8,128)} %param.22) | copy-start | bytes 12292
  173.9 4.9 %copy-start.3 = (s32[128,8]{0,1:T(8,128)S(1)}, s32[128,8]{0,1:T(8,128)}, u32[]{:S(2)}) copy-start(s32[128,8]{0,1:T(8,128)} %param.21) | copy-start | bytes 12292
  173.9 37.8 %all-to-all-start.1 = ((bf16[16,1,48,1024]{3,2,1,0:T(8,128)(2,1)}), bf16[16,1,48,1024]{3,2,1,0:T(8,128)(2,1)}, u32[]{:S(2)}, u32[]{:S(2)}) async-start(bf16[16,1,48,1024]{3,2,1,0:T(8,128)(2,1)} %fusion.24), calls=%async_computation.1 | async-start | bytes 3145728 | tf_op jit(solution)/shard_map/all_to_all | solution.py:134
  178.4 54.3 %reduce-scatter.2.cloned.1.call-start = ((), (), s32[]{:S(2)}) async-start(), calls=%async_computation.3 | async-start | bytes 393216 | tf_op jit(solution)/shard_map/reduce_scatter | solution.py:145
Sparse Core Ops, SparseCore 0:
  223.2 9.4 reduce-scatter.1
